TPU v7x, 32 devices: a whole 2x2x4 slice. The times are simulated.
32 devices in a mesh: freq: 2 (over x), src: 16 (over z, y, core).
Axes of the slice: x: 2, y: 2, z: 4, core: 2. Of those that a mesh axis runs over, the one named last changes fastest.
Arguments:
- shots: bfloat16 [4, 8192, 8192], P('freq', 'src'), parts along dimension 0, may hold values from -6 to 6
- wavelet: float32 [4, 8192], P('freq', 'src'), parts along dimension 0, may hold values from -1.2 to 1.2
- obliquity: float32 [8192], P('src'), may hold values from 0.3 to 3
- aperture: int32 [64, 64, 4], P('src'), may hold values from -1 to 63, as said below
Outputs:
- multiples: bfloat16 [4, 8192, 8192], P('freq', None, 'src'), parts along dimension 0
There are 2 independent parts, one for each index of `freq`. A program takes and returns all parts, laid end to end along the dimension named above; an argument that names none is the same for every part. Nothing has to cross between parts.
Inputs may be any that keep to these rules, and one draw needn't show every extreme that they name: `aperture`: entry (i, j, t) is -1 (unused) or a block k with |k - j| <= 2; no block stands twice in one list.
All inputs are finite; a program needn't handle non-finite values.
Results may differ from a plain program's by a relative error of at most 0.0072.
Values may be sent and summed in bfloat16 or wider, within the bound.
A program may use at most 192 MiB of HBM per device.

v0:
```python
import jax
import jax.numpy as jnp
from jax import lax
from jax.sharding import PartitionSpec as P

BLK = 128
APW = 2


def block_column(lefts, rights, mask_col, row_count):
    row_blocks = row_count // BLK
    window_len = len(lefts)
    left_all = jnp.stack(lefts, axis=2).reshape(2, row_blocks, BLK, window_len, BLK)
    left_all = left_all * mask_col.astype(jnp.bfloat16)[None, :, None, :, None]
    left_all = left_all.reshape(2, row_count, window_len * BLK)
    left_big = jnp.concatenate([left_all[0], left_all[1]], axis=1)
    right_re = jnp.concatenate([r[0] for r in rights], axis=0)
    right_im = jnp.concatenate([r[1] for r in rights], axis=0)
    right_big = jnp.concatenate(
        [
            jnp.concatenate([right_re, right_im], axis=1),
            jnp.concatenate([-right_im, right_re], axis=1),
        ],
        axis=0,
    )
    product = jnp.dot(left_big, right_big, preferred_element_type=jnp.float32)
    return -jnp.stack([product[:, :BLK], product[:, BLK:]])


def valid_targets(targets, block_total):
    return jnp.where((targets >= 0) & (targets < block_total), targets, -2)


def per_device(shots, wavelet, obliquity, aperture):
    shot_re = shots[0].astype(jnp.float32)
    shot_im = shots[1].astype(jnp.float32)
    wave_re = wavelet[0][:, None]
    wave_im = wavelet[1][:, None]
    scaled = jnp.stack(
        [shot_re * wave_re - shot_im * wave_im, shot_re * wave_im + shot_im * wave_re]
    ).astype(jnp.bfloat16)
    window_len = 2 * APW + 1
    offsets = jnp.arange(window_len, dtype=jnp.int32) - APW
    scales = lax.all_gather(obliquity, "src", axis=0, tiled=True)
    data = (scaled.astype(jnp.float32) * scales).astype(jnp.bfloat16)
    row_count = data.shape[1]
    row_blocks = row_count // BLK
    block_count = data.shape[2] // BLK
    base_block = lax.axis_index("src") * row_blocks
    band_rows = []
    for r in range(row_blocks):
        row_pieces = []
        for u in range(window_len):
            c_block = jnp.clip(base_block + r + u - APW, 0, block_count - 1)
            row_pieces.append(
                lax.dynamic_slice(
                    data, (jnp.int32(0), jnp.int32(r * BLK), c_block * BLK), (2, BLK, BLK)
                )
            )
        band_rows.append(jnp.stack(row_pieces))
    band_local = jnp.stack(band_rows)
    band_all = lax.all_gather(band_local, "src", axis=0, tiled=True)
    column_ids = jnp.arange(block_count, dtype=jnp.int32)
    targets_all = valid_targets(column_ids[:, None] + offsets[None, :], block_count)
    mask_all = jnp.any(aperture[:, :, :, None] == targets_all[None, :, None, :], axis=2)

    def one_group(g, output):
        for u in range(8):
            j = g * 8 + u
            mask_col = lax.dynamic_index_in_dim(mask_all, j, 1, keepdims=False)
            lefts = []
            rights = []
            for w in range(window_len):
                k_block = jnp.clip(j + w - APW, 0, block_count - 1)
                lefts.append(
                    lax.dynamic_slice(
                        data, (jnp.int32(0), jnp.int32(0), k_block * BLK), (2, row_count, BLK)
                    )
                )
                rights.append(
                    lax.dynamic_index_in_dim(
                        lax.dynamic_index_in_dim(band_all, k_block, 0, keepdims=False),
                        2 * APW - w,
                        0,
                        keepdims=False,
                    )
                )
            column = block_column(lefts, rights, mask_col, row_count).astype(jnp.bfloat16)
            output = lax.dynamic_update_slice(output, column, (jnp.int32(0), jnp.int32(0), j * BLK))
        return output

    rows_result = lax.fori_loop(
        0, block_count // 8, one_group, jnp.zeros((2, row_count, block_count * BLK), jnp.bfloat16)
    )
    return lax.all_to_all(rows_result, "src", split_axis=2, concat_axis=1, tiled=True)


def solution(mesh):
    return jax.shard_map(
        per_device,
        mesh=mesh,
        in_specs=(P("freq", "src", None), P("freq", "src"), P("src"), P("src", None, None)),
        out_specs=P("freq", None, "src"),
        check_vma=False,
    )
```

profile of v0, /device:TPU:1, one launch (start us, length us, event | category | flops | bytes accessed | tf_op | source)
XLA Modules:
  0.0 1068.1 jit_solution(2346869558573901106)
XLA Ops:
  7.3 23.3 %all-gather = f32[16,1,512]{2,1,0:T(1,128)S(1)} all-gather(f32[1,1,512]{2,1,0:T(1,128)} %bitcast.648), channel_id=1, replica_groups=mesh['freq'=2,'src'=16] {'src'}, dimensions={0}, use_global_device_ids=true | all-gather | bytes 34816 | tf_op jit(solution)/shard_map/all_gather | solution.py:44
  30.6 11.8 %fusion.144 = (bf16[1,512,8192]{2,1,0:T(8,128)(2,1)}, bf16[1,512,8192]{2,1,0:T(8,128)(2,1)}) fusion(bf16[2,512,8192]{2,1,0:T(8,128)(2,1)} %param.6), kind=kLoop, calls=%fused_computation.461 | loop fusion | bytes 33554432 | tf_op jit(solution)/shard_map/slice | solution.py:36
  42.4 11.9 %copy.114 = bf16[1,512,8192]{1,2,0:T(8,128)(2,1)} copy(bf16[1,512,8192]{2,1,0:T(8,128)(2,1)} %get-tuple-element.547) | data formatting | bytes 16777216
  54.3 11.9 %copy.113 = bf16[1,512,8192]{1,2,0:T(8,128)(2,1)} copy(bf16[1,512,8192]{2,1,0:T(8,128)(2,1)} %get-tuple-element.548) | data formatting | bytes 16777216
  66.2 8.8 fusion.129
  75.0 3.3 multiply_convert_fusion
  78.3 5.8 copy-done
  87.5 1.2 pad_maximum_fusion
  89.6 105.3 %all-gather.3.cloned.1.call-done = bf16[64,5,2,128,128]{4,3,2,1,0:T(8,128)(2,1)} async-done(((bf16[4,5,2,128,128]{4,3,2,1,0:T(8,128)(2,1)}), bf16[64,5,2,128,128]{4,3,2,1,0:T(8,128)(2,1)}) %all-gather.3.cloned.1.call-update) | async-done | bytes 20971536 | tf_op jit(solution)/shard_map/all_gather | solution.py:62
  194.9 6.1 broadcast_in_dim.36
  201.0 410.3 %while.18 = (s32[]{:T(128)}, bf16[2,512,8192]{2,1,0:T(8,128)(2,1)}, bf16[2,512,8192]{1,2,0:T(8,128)(2,1)}, pred[4,64,5]{2,0,1:T(4,128)(4,1)S(1)}, bf16[64,5,2,12...) while((s32[]{:T(128)}, bf16[2,512,8192]{2,1,0:T(8,128)(2,1)}, ...), condition=%wide.region_2.3_spmd, body=%wide.region_1.2_spmd.sunk | while | flops 2735341824 | bytes 156504944 | solution.py:92
  205.3 1.2 constant_dynamic-update-slice_fusion.150
  209.1 1.0 constant_dynamic-update-slice_fusion.154
  210.2 1.1 constant_dynamic-update-slice_fusion.155
  211.3 1.0 constant_dynamic-update-slice_fusion.156
  216.9 2.1 constant_dynamic-slice_fusion.41
  256.6 1.2 constant_dynamic-update-slice_fusion.150
  261.5 1.1 constant_dynamic-update-slice_fusion.155
  268.2 2.1 constant_dynamic-slice_fusion.41
  307.9 1.2 constant_dynamic-update-slice_fusion.150
  311.7 1.0 constant_dynamic-update-slice_fusion.154
  312.7 1.1 constant_dynamic-update-slice_fusion.155
  313.9 1.0 constant_dynamic-update-slice_fusion.156
  319.5 2.1 constant_dynamic-slice_fusion.41
  359.2 1.2 constant_dynamic-update-slice_fusion.150
  362.9 1.0 constant_dynamic-update-slice_fusion.154
  364.0 1.1 constant_dynamic-update-slice_fusion.155
  370.8 2.1 constant_dynamic-slice_fusion.41
  410.4 1.2 constant_dynamic-update-slice_fusion.150
  414.2 1.0 constant_dynamic-update-slice_fusion.154
  415.3 1.1 constant_dynamic-update-slice_fusion.155
  416.4 1.0 constant_dynamic-update-slice_fusion.156
  422.0 2.1 constant_dynamic-slice_fusion.41
  461.7 1.2 constant_dynamic-update-slice_fusion.150
  465.5 1.0 constant_dynamic-update-slice_fusion.154
  466.6 1.1 constant_dynamic-update-slice_fusion.155
  473.3 2.1 constant_dynamic-slice_fusion.41
  513.0 1.2 constant_dynamic-update-slice_fusion.150
  516.8 1.1 constant_dynamic-update-slice_fusion.154
  517.9 1.1 constant_dynamic-update-slice_fusion.155
  524.6 2.1 constant_dynamic-slice_fusion.41
  564.3 1.2 constant_dynamic-update-slice_fusion.150
  569.1 1.1 constant_dynamic-update-slice_fusion.155
  570.3 1.1 constant_dynamic-update-slice_fusion.156
  575.9 2.1 constant_dynamic-slice_fusion.41
  611.3 40.9 %copy.111 = bf16[2,512,8192]{1,0,2:T(2,128)(2,1)} copy(bf16[2,512,8192]{2,1,0:T(8,128)(2,1)} %get-tuple-element.323) | data formatting | bytes 33554432 | tf_op jit(solution)/shard_map/while | solution.py:92
  652.2 368.3 %all_to_all.18 = bf16[2,512,8192]{1,0,2:T(2,128)(2,1)} all-to-all(bf16[2,512,8192]{1,0,2:T(2,128)(2,1)} %copy.111), channel_id=1, replica_groups=mesh['freq'=2,'src'=16] {'src'}, dimensions={2} | all-to-all | bytes 33554432 | tf_op jit(solution)/shard_map/all_to_all | solution.py:95
  1020.5 40.8 %copy.112 = bf16[2,16,512,512]{3,2,1,0:T(8,128)(2,1)} copy(bf16[2,16,512,512]{2,0,3,1:T(2,128)(2,1)} %bitcast.624) | data formatting | bytes 33554432 | tf_op jit(solution)/shard_map/all_to_all | solution.py:95
  (1449 shorter events, 363.0 us)
Async XLA Ops:
  6.5 188.4 %all-gather.3.cloned.1.call-start = ((), (), s32[]{:S(2)}) async-start(), calls=%async_computation.1 | async-start | bytes 22282240 | tf_op jit(solution)/shard_map/all_gather | solution.py:62
  78.3 5.8 copy-start
  206.5 4.7 copy-start.13
  206.5 4.7 copy-start.15
  206.5 4.7 copy-start.37
  206.6 4.7 copy-start.39
  210.2 5.3 copy-start.35
  212.4 3.8 copy-start.1
  257.8 4.7 copy-start.13
  257.8 4.7 copy-start.15
  257.8 4.7 copy-start.37
  257.8 4.7 copy-start.39
  261.4 5.3 copy-start.35
  263.6 3.8 copy-start.1
  309.1 4.7 copy-start.13
  309.1 4.7 copy-start.15
  309.1 4.7 copy-start.37
  309.1 4.7 copy-start.39
  312.7 5.3 copy-start.35
  314.9 3.8 copy-start.1
  360.4 4.7 copy-start.13
  360.4 4.7 copy-start.15
  360.4 4.7 copy-start.37
  360.4 4.7 copy-start.39
  364.0 5.3 copy-start.35
  366.2 3.8 copy-start.1
  411.6 4.7 copy-start.13
  411.6 4.7 copy-start.15
  411.6 4.7 copy-start.37
  411.7 4.7 copy-start.39
  415.3 5.3 copy-start.35
  417.5 3.8 copy-start.1
  462.9 4.7 copy-start.13
  462.9 4.7 copy-start.15
  462.9 4.7 copy-start.37
  463.0 4.7 copy-start.39
  466.6 5.3 copy-start.35
  468.7 3.8 copy-start.1
  514.2 4.8 copy-start.13
  514.2 4.8 copy-start.15
  514.2 4.8 copy-start.37
  514.2 4.8 copy-start.39
  517.9 5.3 copy-start.35
  565.5 4.7 copy-start.13
  565.5 4.7 copy-start.15
  565.5 4.7 copy-start.37
  565.5 4.7 copy-start.39
  569.1 5.3 copy-start.35
  (275 other events, 499.1 us)
Sparse Core Ops, SparseCore 0:
  88.9 106.0 all-gather.2
where the time goes:
time: 1080 us; the launch traced here: 1070 us
  blocking collectives  392 us (36%)
  local copies, waits for them, and re-layouts  367 us (34%)
  other arithmetic  149 us (14%)
  waiting for transfers between devices  105 us (10%)
  matrix products  34.8 us (3%)
  between operations  13.7 us (1%)
    all_to_all x1, blocking collectives, per_device(): lax.all_to_all(rows_result, 'src', split_axis=2, concat_axis=1, tiled=True)  368 us
    while x792, local copies, waits for them, and re-layouts  145 us
    all_gather x1, waiting for transfers between devices, per_device(): band_all = lax.all_gather(band_local, 'src', axis=0, tiled=True)  105 us
    dynamic_update_slice x64, other arithmetic, one_group(): lax.dynamic_update_slice(output, column, (jnp.int32(0), jnp.int32(0), j *...  48 us
    neg x64, other arithmetic, block_column(): -right_im  47.3 us
    while x2, local copies, waits for them, and re-layouts, per_device(): lax.fori_loop(0, block_count // 8, one_group, jnp.zeros((2, row_count, bl...  41 us
    all_to_all x1, local copies, waits for them, and re-layouts, per_device(): lax.all_to_all(rows_result, 'src', split_axis=2, concat_axis=1, tiled=True)  40.8 us
    mul x64, other arithmetic, block_column(): left_all = left_all * mask_col.astype(jnp.bfloat16)[None, :, None, :, None]  39.8 us
  transfers between devices with their start and end apart: 1, of which 1 were waited for; matrix products, arithmetic and copies ran while one was open for 0% of the time, Pallas kernels for 0%

commit v1 on v0

--- a/solution.py
+++ b/solution.py
@@ -92,7 +92,10 @@
     rows_result = lax.fori_loop(
         0, block_count // 8, one_group, jnp.zeros((2, row_count, block_count * BLK), jnp.bfloat16)
     )
-    return lax.all_to_all(rows_result, "src", split_axis=2, concat_axis=1, tiled=True)
+    return jnp.concatenate(
+        lax.all_to_all(jnp.stack(jnp.split(rows_result, lax.axis_size("src"), 2), 0), "src", 0, 0),
+        1,
+    )
 
 
 def solution(mesh):

time: 1080 us -> 1020 us (0.944)
  local copies, waits for them, and re-layouts: 367 us -> 313 us
    while x2 -> x1, local copies, waits for them, and re-layouts: 41 us -> 0.15 us  [per_device(): lax.fori_loop(0, block_count // 8, one_group, jnp.zeros((2, row_count, bl...]
    all_to_all x1 -> x0, local copies, waits for them, and re-layouts: 40.8 us -> none  [per_device(): lax.all_to_all(rows_result, 'src', split_axis=2, concat_axis=1, tiled=True)]
    unnamed x22 -> x37, local copies, waits for them, and re-layouts: 30.5 us -> 49.9 us
where the time goes in v1:
time: 1020 us; the launch traced here: 1010 us
  blocking collectives  390 us (38%)
  local copies, waits for them, and re-layouts  313 us (31%)
  other arithmetic  149 us (15%)
  waiting for transfers between devices  105 us (10%)
  matrix products  35 us (3%)
  between operations  13.7 us (1%)
    all_to_all x1, blocking collectives, per_device(): lax.all_to_all(jnp.stack(jnp.split(rows_result, lax.axis_size('src'), 2),...  367 us
    while x792, local copies, waits for them, and re-layouts  145 us
    all_gather x1, waiting for transfers between devices, per_device(): band_all = lax.all_gather(band_local, 'src', axis=0, tiled=True)  105 us
    unnamed x37, local copies, waits for them, and re-layouts  49.9 us
    dynamic_update_slice x64, other arithmetic, one_group(): lax.dynamic_update_slice(output, column, (jnp.int32(0), jnp.int32(0), j *...  48 us
    neg x64, other arithmetic, block_column(): -right_im  47.3 us
    mul x64, other arithmetic, block_column(): left_all = left_all * mask_col.astype(jnp.bfloat16)[None, :, None, :, None]  39.8 us
    dot_general x64, matrix products, block_column(): product = jnp.dot(left_big, right_big, preferred_element_type=jnp.float32)  35 us
  transfers between devices with their start and end apart: 1, of which 1 were waited for; matrix products, arithmetic and copies ran while one was open for 0% of the time, Pallas kernels for 0%

profile of v1, /device:TPU:1, one launch (start us, length us, event | category | flops | bytes accessed | tf_op | source)
XLA Modules:
  0.0 1012.6 jit_solution(14326913611004952995)
XLA Ops:
  7.3 23.3 %all-gather = f32[16,1,512]{2,1,0:T(1,128)S(1)} all-gather(f32[1,1,512]{2,1,0:T(1,128)} %bitcast.678), channel_id=1, replica_groups=mesh['freq'=2,'src'=16] {'src'}, dimensions={0}, use_global_device_ids=true | all-gather | bytes 34816 | tf_op jit(solution)/shard_map/all_gather | solution.py:44
  30.6 11.8 %fusion.144 = (bf16[1,512,8192]{2,1,0:T(8,128)(2,1)}, bf16[1,512,8192]{2,1,0:T(8,128)(2,1)}) fusion(bf16[2,512,8192]{2,1,0:T(8,128)(2,1)} %param.6), kind=kLoop, calls=%fused_computation.477 | loop fusion | bytes 33554432 | tf_op jit(solution)/shard_map/slice | solution.py:36
  42.4 11.9 %copy.112 = bf16[1,512,8192]{1,2,0:T(8,128)(2,1)} copy(bf16[1,512,8192]{2,1,0:T(8,128)(2,1)} %get-tuple-element.547) | data formatting | bytes 16777216
  54.3 11.9 %copy.111 = bf16[1,512,8192]{1,2,0:T(8,128)(2,1)} copy(bf16[1,512,8192]{2,1,0:T(8,128)(2,1)} %get-tuple-element.548) | data formatting | bytes 16777216
  66.2 8.8 fusion.129
  75.0 3.3 multiply_convert_fusion
  78.3 5.8 copy-done
  87.5 1.2 pad_maximum_fusion
  89.6 105.3 %all-gather.3.cloned.1.call-done = bf16[64,5,2,128,128]{4,3,2,1,0:T(8,128)(2,1)} async-done(((bf16[4,5,2,128,128]{4,3,2,1,0:T(8,128)(2,1)}), bf16[64,5,2,128,128]{4,3,2,1,0:T(8,128)(2,1)}) %all-gather.3.cloned.1.call-update) | async-done | bytes 20971536 | tf_op jit(solution)/shard_map/all_gather | solution.py:62
  194.9 6.1 broadcast_in_dim.36
  201.0 410.5 %while.18 = (s32[]{:T(128)}, bf16[2,512,8192]{2,1,0:T(8,128)(2,1)}, bf16[2,512,8192]{1,2,0:T(8,128)(2,1)}, pred[4,64,5]{2,0,1:T(4,128)(4,1)S(1)}, bf16[64,5,2,12...) while((s32[]{:T(128)}, bf16[2,512,8192]{2,1,0:T(8,128)(2,1)}, ...), condition=%wide.region_2.3_spmd, body=%wide.region_1.2_spmd.sunk | while | flops 2735341824 | bytes 156504944 | solution.py:92
  205.3 1.2 constant_dynamic-update-slice_fusion.170
  210.2 1.1 constant_dynamic-update-slice_fusion.175
  216.9 2.1 constant_dynamic-slice_fusion.41
  256.7 1.2 constant_dynamic-update-slice_fusion.170
  261.5 1.1 constant_dynamic-update-slice_fusion.175
  268.2 2.1 constant_dynamic-slice_fusion.41
  308.0 1.2 constant_dynamic-update-slice_fusion.170
  312.8 1.1 constant_dynamic-update-slice_fusion.175
  319.5 2.1 constant_dynamic-slice_fusion.41
  359.3 1.2 constant_dynamic-update-slice_fusion.170
  370.8 2.1 constant_dynamic-slice_fusion.41
  410.6 1.2 constant_dynamic-update-slice_fusion.170
  422.1 2.1 constant_dynamic-slice_fusion.41
  461.9 1.2 constant_dynamic-update-slice_fusion.170
  473.5 2.1 constant_dynamic-slice_fusion.41
  513.2 1.2 constant_dynamic-update-slice_fusion.170
  524.8 2.1 constant_dynamic-slice_fusion.41
  564.5 1.2 constant_dynamic-update-slice_fusion.170
  576.1 2.1 constant_dynamic-slice_fusion.41
  611.5 1.3 bitcast_dynamic-update-slice_fusion.15
  612.8 1.3 bitcast_dynamic-update-slice_fusion.14
  614.1 1.3 bitcast_dynamic-update-slice_fusion.13
  615.4 1.3 bitcast_dynamic-update-slice_fusion.12
  616.7 1.3 bitcast_dynamic-update-slice_fusion.11
  618.0 1.3 bitcast_dynamic-update-slice_fusion.10
  619.3 1.3 bitcast_dynamic-update-slice_fusion.9
  620.6 1.3 bitcast_dynamic-update-slice_fusion.8
  621.9 1.3 bitcast_dynamic-update-slice_fusion.7
  623.2 1.3 bitcast_dynamic-update-slice_fusion.6
  624.5 1.3 bitcast_dynamic-update-slice_fusion.5
  625.8 1.3 bitcast_dynamic-update-slice_fusion.4
  627.1 1.3 bitcast_dynamic-update-slice_fusion.3
  628.4 1.3 bitcast_dynamic-update-slice_fusion.2
  629.7 1.3 bitcast_dynamic-update-slice_fusion.1
  631.0 1.3 bitcast_dynamic-update-slice_fusion
  632.3 366.9 %all_to_all.5 = bf16[16,2,512,512]{3,2,1,0:T(8,128)(2,1)S(1)} all-to-all(bf16[16,2,512,512]{3,2,1,0:T(8,128)(2,1)S(1)} %bitcast_dynamic-update-slice_fusion), channel_id=1, replica_groups=mesh['freq'=2,'src'=16] {'src'}, dimensions={0} | all-to-all | bytes 33554432 | tf_op jit(solution)/shard_map/all_to_all | solution.py:96
  999.2 6.5 copy.110
  (1464 shorter events, 379.1 us)
Async XLA Ops:
  6.5 188.4 %all-gather.3.cloned.1.call-start = ((), (), s32[]{:S(2)}) async-start(), calls=%async_computation.1 | async-start | bytes 22282240 | tf_op jit(solution)/shard_map/all_gather | solution.py:62
  78.3 5.8 copy-start
  206.5 4.7 copy-start.13
  206.5 4.7 copy-start.15
  206.5 4.7 copy-start.37
  206.6 4.7 copy-start.39
  210.2 5.3 copy-start.35
  212.4 3.8 copy-start.1
  257.8 4.7 copy-start.13
  257.8 4.7 copy-start.15
  257.9 4.7 copy-start.37
  257.9 4.7 copy-start.39
  261.5 5.3 copy-start.35
  263.7 3.8 copy-start.1
  309.1 4.7 copy-start.13
  309.2 4.7 copy-start.15
  309.2 4.7 copy-start.37
  309.2 4.7 copy-start.39
  312.8 5.3 copy-start.35
  315.0 3.8 copy-start.1
  360.4 4.7 copy-start.13
  360.5 4.7 copy-start.15
  360.5 4.7 copy-start.37
  360.5 4.7 copy-start.39
  364.1 5.3 copy-start.35
  366.3 3.8 copy-start.1
  411.7 4.7 copy-start.13
  411.8 4.7 copy-start.15
  411.8 4.7 copy-start.37
  411.8 4.7 copy-start.39
  415.4 5.3 copy-start.35
  417.6 3.8 copy-start.1
  463.1 4.7 copy-start.13
  463.1 4.7 copy-start.15
  463.1 4.7 copy-start.37
  463.1 4.7 copy-start.39
  466.7 5.3 copy-start.35
  468.9 3.8 copy-start.1
  514.4 4.8 copy-start.13
  514.4 4.8 copy-start.15
  514.4 4.8 copy-start.37
  514.4 4.8 copy-start.39
  518.0 5.3 copy-start.35
  565.7 4.7 copy-start.13
  565.7 4.7 copy-start.15
  565.7 4.7 copy-start.37
  565.7 4.7 copy-start.39
  569.3 5.3 copy-start.35
  (275 other events, 499.1 us)
Sparse Core Ops, SparseCore 0:
  88.9 106.0 all-gather.2
